TPU v7x, 256 devices: a whole 4x4x8 slice. The times are simulated.
256 devices in a mesh: gx: 8 (over y, core), gy: 4 (over z_lo), gz: 8 (over z_hi, x).
Axes of the slice: x: 4, y: 4, z: 8 (z_hi: 2, z_lo: 4; z = z_hi * 4 + z_lo), core: 2. Of those that a mesh axis runs over, the one named last changes fastest.
Arguments:
- tokens: bfloat16 [2048, 8192], P(('gx', 'gy'), 'gz'), may hold values from -6 to 6
- gate_weight: bfloat16 [8192, 28672], P('gz', ('gx', 'gy')), may hold values from -0.0625 to 0.0625
- up_weight: bfloat16 [8192, 28672], P('gz', ('gx', 'gy')), may hold values from -0.0625 to 0.0625
- down_weight: bfloat16 [28672, 8192], P(('gx', 'gy'), 'gz'), may hold values from -0.03125 to 0.03125
Outputs:
- layer_output: bfloat16 [2048, 8192], P(('gx', 'gy'), 'gz')
All inputs are finite; a program needn't handle non-finite values.
Results may differ from a plain program's by a relative error of at most 0.029.
Values may be sent and summed in bfloat16 or wider, within the bound.
A program may use at most 128 MiB of HBM per device.

v0:
```python
import jax
import jax.numpy as jnp
from jax import lax
from jax.sharding import PartitionSpec as P


def shards(tokens, gate_weight, up_weight, down_weight):
    gathered = lax.all_gather(tokens, "gx", axis=0, tiled=True)

    def column_product(weight_piece):
        return jnp.dot(gathered, weight_piece, preferred_element_type=jnp.float32)

    gate_partial = column_product(lax.all_gather(gate_weight, "gy", axis=1, tiled=True))
    up_partial = column_product(lax.all_gather(up_weight, "gy", axis=1, tiled=True))
    gate_sum, up_sum = (
        lax.psum_scatter(
            gate_partial.astype(jnp.bfloat16), "gz", scatter_dimension=0, tiled=True
        ).astype(jnp.float32),
        lax.psum_scatter(
            up_partial.astype(jnp.bfloat16), "gz", scatter_dimension=0, tiled=True
        ).astype(jnp.float32),
    )
    local_hidden = (jax.nn.silu(gate_sum) * up_sum).astype(jnp.bfloat16)
    hidden = lax.all_gather(local_hidden, "gz", axis=0, tiled=True)
    down_partial = jnp.dot(
        hidden,
        lax.all_gather(down_weight, "gy", axis=0, tiled=True),
        preferred_element_type=jnp.float32,
    )
    layer_output = lax.psum_scatter(
        down_partial.astype(jnp.bfloat16), "gx", scatter_dimension=0, tiled=True
    )
    return layer_output


def solution(mesh):
    return jax.shard_map(
        shards,
        mesh=mesh,
        in_specs=(
            P(("gx", "gy"), "gz"),
            P("gz", ("gx", "gy")),
            P("gz", ("gx", "gy")),
            P(("gx", "gy"), "gz"),
        ),
        out_specs=P(("gx", "gy"), "gz"),
        check_vma=False,
    )
```

profile of v0, /device:TPU:1, one launch (start us, length us, event | category | flops | bytes accessed | tf_op | source)
XLA Modules:
  0.0 837.7 jit_solution(120754620333667691)
XLA Ops:
  6.5 0.7 all-gather.6.cloned.1.call-update
  7.3 0.0 all-gather.8.cloned.1.call-start
  7.3 0.7 all-gather.8.cloned.1.call-update
  8.0 0.0 all-gather.10.cloned.1.call-start
  8.1 0.7 all-gather.10.cloned.1.call-update
  8.7 0.0 reduce-scatter.4.cloned.1.call-start
  8.8 30.6 %all-gather.6.cloned.1.call-done = bf16[512,1024]{1,0:T(8,128)(2,1)} async-done(((bf16[64,1024]{1,0:T(8,128)(2,1)}), bf16[512,1024]{1,0:T(8,128)(2,1)}) %all-gather.6.cloned.1.call-update) | async-done | bytes 1048592 | tf_op jit(solution)/shard_map/all_gather | solution.py:8
  39.4 137.1 %all-gather.8.cloned.1.call-done = bf16[1024,3584]{1,0:T(8,128)(2,1)} async-done(((bf16[1024,896]{1,0:T(8,128)(2,1)}), bf16[1024,3584]{1,0:T(8,128)(2,1)}) %all-gather.8.cloned.1.call-update) | async-done | bytes 7340048 | tf_op jit(solution)/shard_map/all_gather | solution.py:13
  176.5 9.2 %convolution_convert_fusion.1 = bf16[512,3584]{1,0:T(8,128)(2,1)} fusion(bf16[512,1024]{1,0:T(8,128)(2,1)} %all-gather.6.cloned.1.call-done, bf16[1024,3584]{1,0:T(8,128)(2,1)} %all-gather.8.cloned.1.call-done), kind=kOutput, calls=%fused_computation.1 | convolution fusion | flops 3759931392 | bytes 12058624 | tf_op jit(solution)/shard_map/dot_general | solution.py:11
  185.8 0.0 reduce-scatter.4.cloned.1.call-update
  185.8 0.0 reduce-scatter.6.cloned.1.call-start
  185.8 128.1 %all-gather.10.cloned.1.call-done = bf16[1024,3584]{1,0:T(8,128)(2,1)} async-done(((bf16[1024,896]{1,0:T(8,128)(2,1)}), bf16[1024,3584]{1,0:T(8,128)(2,1)}) %all-gather.10.cloned.1.call-update) | async-done | bytes 7340048 | tf_op jit(solution)/shard_map/all_gather | solution.py:14
  313.9 8.4 %convolution_convert_fusion = bf16[512,3584]{1,0:T(8,128)(2,1)} fusion(bf16[512,1024]{1,0:T(8,128)(2,1)S(1)} %copy-done, bf16[1024,3584]{1,0:T(8,128)(2,1)} %all-gather.10.cloned.1.call-done), kind=kOutput, calls=%fused_computation | convolution fusion | flops 3759931392 | bytes 12058624 | tf_op jit(solution)/shard_map/dot_general | solution.py:11
  322.4 0.0 all-gather.14.cloned.1.call-start
  322.5 0.5 all-gather.14.cloned.1.call-update
  323.0 0.0 all-gather.12.cloned.1.call-start
  323.0 114.3 %reduce-scatter.4.cloned.1.call-done = bf16[64,3584]{1,0:T(8,128)(2,1)} async-done(((bf16[512,3584]{1,0:T(8,128)(2,1)}), bf16[64,3584]{1,0:T(8,128)(2,1)}) %reduce-scatter.4.cloned.1.call-update) | async-done | bytes 458768 | tf_op jit(solution)/shard_map/reduce_scatter | solution.py:16
  437.4 121.3 %reduce-scatter.6.cloned.1.call-done = bf16[64,3584]{1,0:T(8,128)(2,1)} async-done(((bf16[512,3584]{1,0:T(8,128)(2,1)}), bf16[64,3584]{1,0:T(8,128)(2,1)}) %reduce-scatter.6.cloned.1.call-update) | async-done | bytes 458768 | tf_op jit(solution)/shard_map/reduce_scatter | solution.py:19
  558.6 2.2 fusion.4
  560.9 0.0 reduce-scatter.8.cloned.1.call-start
  560.9 132.2 %all-gather.14.cloned.1.call-done = bf16[3584,1024]{1,0:T(8,128)(2,1)} async-done(((bf16[896,1024]{1,0:T(8,128)(2,1)}), bf16[3584,1024]{1,0:T(8,128)(2,1)}) %all-gather.14.cloned.1.call-update) | async-done | bytes 7340048 | tf_op jit(solution)/shard_map/all_gather | solution.py:27
  693.1 101.3 %all-gather.12.cloned.1.call-done = bf16[512,3584]{1,0:T(8,128)(2,1)} async-done(((bf16[64,3584]{1,0:T(8,128)(2,1)}), bf16[512,3584]{1,0:T(8,128)(2,1)}) %all-gather.12.cloned.1.call-update) | async-done | bytes 3670032 | tf_op jit(solution)/shard_map/all_gather | solution.py:24
  794.5 9.1 %convolution_convert_fusion.2 = bf16[512,1024]{1,0:T(8,128)(2,1)} fusion(bf16[512,3584]{1,0:T(8,128)(2,1)} %all-gather.12.cloned.1.call-done, bf16[3584,1024]{1,0:T(8,128)(2,1)} %all-gather.14.cloned.1.call-done), kind=kOutput, calls=%fused_computation.2 | convolution fusion | flops 3758620672 | bytes 12058624 | tf_op jit(solution)/shard_map/dot_general | solution.py:25
  803.6 27.3 %reduce-scatter.8.cloned.1.call-done = bf16[64,1024]{1,0:T(8,128)(2,1)} async-done(((bf16[512,1024]{1,0:T(8,128)(2,1)}), bf16[64,1024]{1,0:T(8,128)(2,1)}) %reduce-scatter.8.cloned.1.call-update) | async-done | bytes 131088 | tf_op jit(solution)/shard_map/reduce_scatter | solution.py:30
  (6 shorter events, 0.1 us)
Async XLA Ops:
  6.5 32.9 %all-gather.6.cloned.1.call-start = ((), (), s32[]{:S(2)}) async-start(), calls=%async_computation.3 | async-start | bytes 1179648 | tf_op jit(solution)/shard_map/all_gather | solution.py:8
  7.3 169.3 %all-gather.8.cloned.1.call-start = ((), (), s32[]{:S(2)}) async-start(), calls=%async_computation.4 | async-start | bytes 9175040 | tf_op jit(solution)/shard_map/all_gather | solution.py:13
  8.0 305.9 %all-gather.10.cloned.1.call-start = ((), (), s32[]{:S(2)}) async-start(), calls=%async_computation.6 | async-start | bytes 9175040 | tf_op jit(solution)/shard_map/all_gather | solution.py:14
  8.7 428.6 %reduce-scatter.4.cloned.1.call-start = ((), (), s32[]{:S(2)}) async-start(), calls=%async_computation.5 | async-start | bytes 4128768 | tf_op jit(solution)/shard_map/reduce_scatter | solution.py:16
  39.4 274.5 %copy-start = (bf16[512,1024]{1,0:T(8,128)(2,1)S(1)}, bf16[512,1024]{1,0:T(8,128)(2,1)}, u32[]{:S(2)}) copy-start(bf16[512,1024]{1,0:T(8,128)(2,1)} %all-gather.6.cloned.1.call-done) | copy-start | bytes 3145732
  185.8 372.9 %reduce-scatter.6.cloned.1.call-start = ((), (), s32[]{:S(2)}) async-start(), calls=%async_computation.7 | async-start | bytes 4128768 | tf_op jit(solution)/shard_map/reduce_scatter | solution.py:19
  322.4 370.7 %all-gather.14.cloned.1.call-start = ((), (), s32[]{:S(2)}) async-start(), calls=%async_computation.9 | async-start | bytes 9175040 | tf_op jit(solution)/shard_map/all_gather | solution.py:27
  323.0 471.5 %all-gather.12.cloned.1.call-start = ((), (), s32[]{:S(2)}) async-start(), calls=%async_computation.8 | async-start | bytes 4128768 | tf_op jit(solution)/shard_map/all_gather | solution.py:24
  560.9 270.0 %reduce-scatter.8.cloned.1.call-start = ((), (), s32[]{:S(2)}) async-start(), calls=%async_computation.10 | async-start | bytes 1179648 | tf_op jit(solution)/shard_map/reduce_scatter | solution.py:30
Sparse Core Ops, SparseCore 0:
  9.2 30.1 all-gather.5
  41.2 135.2 all-gather.7
  178.4 135.5 all-gather.9
  318.1 119.2 reduce-scatter.3
  442.1 116.5 reduce-scatter.5
  560.3 132.7 all-gather.13
  695.7 98.6 all-gather.11
  803.7 27.0 reduce-scatter.7
where the time goes:
time: 839 us; the launch traced here: 838 us
  waiting for transfers between devices  795 us (95%)
  matrix products  26.8 us (3%)
  between operations  13.5 us (2%)
    all_gather x1, waiting for transfers between devices, shards(): lax.all_gather(gate_weight, 'gy', axis=1, tiled=True)  137 us
    all_gather x1, waiting for transfers between devices, shards(): lax.all_gather(down_weight, 'gy', axis=0, tiled=True)  132 us
    all_gather x1, waiting for transfers between devices, shards(): lax.all_gather(up_weight, 'gy', axis=1, tiled=True)  128 us
    reduce_scatter x1, waiting for transfers between devices, shards(): lax.psum_scatter(up_partial.astype(jnp.bfloat16), 'gz', scatter_dimension...  121 us
    reduce_scatter x1, waiting for transfers between devices, shards(): lax.psum_scatter(gate_partial.astype(jnp.bfloat16), 'gz', scatter_dimensi...  114 us
    all_gather x1, waiting for transfers between devices, shards(): hidden = lax.all_gather(local_hidden, 'gz', axis=0, tiled=True)  101 us
    all_gather x1, waiting for transfers between devices, shards(): gathered = lax.all_gather(tokens, 'gx', axis=0, tiled=True)  30.6 us
    reduce_scatter x1, waiting for transfers between devices, shards(): lax.psum_scatter(down_partial.astype(jnp.bfloat16), 'gx', scatter_dimensi...  27.3 us
  transfers between devices with their start and end apart: 8, of which 8 were waited for; matrix products, arithmetic and copies ran while one was open for 2% of the time, Pallas kernels for 0%

commit v1 on v0

v1 whole, which is shorter than its diff:
```python
import functools

import jax
import jax.numpy as jnp
from jax import lax
from jax.experimental import pallas as pl
from jax.experimental.pallas import tpu as pltpu
from jax.sharding import PartitionSpec as P

PANELS = 4
BF16, F32 = jnp.bfloat16, jnp.float32
STEPS = ("A1", "A2", "A3", "A4", "M1", "X2", "Z1", "H", "E2", "E3", "M2", "G2", "G3", "G4", "G5")
COPIES = (
    "az1", "az2", "az3", "ayr", "ayl", "arr", "arl", "ac",
    "s1g", "s1u", "sug", "sgu", "lg", "lu", "z",
    "ez", "eor", "eol", "epr", "epl", "err", "erl",
    "gc", "y1a", "y1b", "ysb", "ysa", "yla", "ylb", "gz1", "gz2", "gz3",
)
SEM = {name: i for i, name in enumerate(COPIES)}


def step_order(panels):
    f = 4.0 / panels
    lat = 1.5
    table = dict(
        A1=((), 0.1, (("az", "z", 2.3),)),
        A2=(("az",), 0.1, (("ay", "y", 2.9),)),
        A3=(("ay",), 0.1, (("ar", "y", 1.5),)),
        A4=(("ar",), 0.1, (("ac", "c", 1.0),)),
        M1=(("ac",), 2.5, (("s1", "x", 5.0), ("sh", "x", 5.0))),
        X2=(("s1",), 0.5, (("lo", "x", 5.0),)),
        Z1=(("lo", "sh"), 1.0, (("zz", "z", 10.0),)),
        H=(("zz",), 1.0, (("ez", "z", 5.0), ("eo", "x", 2.5))),
        E2=(("ez",), 0.1, (("ep", "x", 2.5),)),
        E3=(("eo", "ep"), 0.1, (("er", "x", 2.5),)),
        M2=(("er",), 1.5, (("gc", "c", 1.0),)),
        G2=(("gc",), 1.0, (("y1", "y", 1.4), ("ys", "y", 1.4))),
        G3=(("y1",), 0.3, (("yl", "y", 1.4),)),
        G4=(("yl", "ys"), 0.5, (("gz", "z", 2.5),)),
        G5=(("gz",), 0.3, ()),
    )
    done, arrive, free = {}, {}, dict(x=0.0, y=0.0, z=0.0, c=0.0)
    now, order = 0.0, []
    while len(order) < panels * len(STEPS):
        best = None
        for p in range(panels):
            for i, s in enumerate(STEPS):
                if (p, s) in done:
                    continue
                if i and (p, STEPS[i - 1]) not in done:
                    break
                if p and (p - 1, s) not in done:
                    break
                if p and s == "M1" and (p - 1, "X2") not in done:
                    break
                ready = max([arrive[(p, m)] for m in table[s][0]] + [0.0])
                key = (max(ready, now), -i)
                if best is None or key < best[0]:
                    best = (key, p, s)
                break
        (start, _), p, s = best
        now = start + table[s][1] * f
        for name, link, time in table[s][2]:
            free[link] = max(free[link], now) + time * f
            arrive[(p, name)] = free[link] + lat
        done[(p, s)] = now
        order.append((p, s))
    return tuple(order)


def kernel(
    panels, tokens, gate_hbm, up_hbm, down_hbm, out,
    wgu, wd, tok, part, s1g, s1u, lg, sgu, lu, sug, zsend, zkeep, zrecv, hid, outp,
    crecv, osum, y1a, y1b, yla, ysa, ylb, ysb, zos, zor, send_sem, recv_sem, weight_sem,
):
    gx, gy, gz = lax.axis_index("gx"), lax.axis_index("gy"), lax.axis_index("gz")
    x, h, y, c, zl = lax.rem(gz, 4), gz // 4, gx // 2, lax.rem(gx, 2), gy
    r = 64 // panels
    rows = 4 * r
    half = rows // 2
    ff = gate_hbm.shape[1]
    mid = out.shape[1] // 2

    def mod4(v):
        return lax.rem(v + 4, 4)

    def device(x=x, h=h, y=y, c=c, zl=zl):
        return {"gx": 2 * y + c, "gy": zl, "gz": 4 * h + x}

    xr, xl = device(x=mod4(x + 1)), device(x=mod4(x - 1))
    yr, yl = device(y=mod4(y + 1)), device(y=mod4(y - 1))
    zpeer = device(h=1 - h)
    core = device(c=1 - c)
    zs = [None] + [device(zl=mod4(zl + k)) for k in (1, 2, 3)]

    barrier = pltpu.get_barrier_semaphore()
    peers = (xr, xl, yr, yl, zpeer, core, zs[1], zs[2], zs[3])
    for peer in peers:
        pl.semaphore_signal(barrier, inc=1, device_id=peer, device_id_type=pl.DeviceIdType.MESH)
    loads = [
        pltpu.make_async_copy(gate_hbm, wgu.at[:, pl.ds(0, ff)], weight_sem.at[0]),
        pltpu.make_async_copy(up_hbm, wgu.at[:, pl.ds(ff, ff)], weight_sem.at[1]),
        pltpu.make_async_copy(down_hbm, wd, weight_sem.at[2]),
    ]
    for load in loads:
        load.start()
    cy = 4 * c + y
    for p in range(panels):
        tok[p, cy, zl] = tokens[pl.ds(p * r, r), :]
    pl.semaphore_wait(barrier, len(peers))

    sent = []

    def send(p, name, src, dst, to):
        copy = pltpu.make_async_remote_copy(
            src_ref=src, dst_ref=dst, send_sem=send_sem.at[p, SEM[name]],
            recv_sem=recv_sem.at[p, SEM[name]], device_id=to, device_id_type=pl.DeviceIdType.MESH,
        )
        copy.start()
        sent.append(copy)

    def arrived(p, name, dst):
        pltpu.make_async_remote_copy(
            src_ref=dst, dst_ref=dst, send_sem=send_sem.at[p, SEM[name]],
            recv_sem=recv_sem.at[p, SEM[name]], device_id=core, device_id_type=pl.DeviceIdType.MESH,
        ).wait_recv()

    g, u = pl.ds(0, ff), pl.ds(ff, ff)
    ca, cb = pl.ds(0, mid), pl.ds(mid, mid)

    def two(j):
        return pl.ds(2 * mod4(j), 2)

    def f32(v):
        return v.astype(F32)

    def a1(p):
        for k in (1, 2, 3):
            here = tok.at[p, cy, zl]
            send(p, "az%d" % k, here, here, zs[k])

    def a2(p):
        for k in (1, 2, 3):
            arrived(p, "az%d" % k, tok.at[p, cy, mod4(zl - k)])
        here = tok.at[p, cy]
        send(p, "ayr", here, here, yr)
        send(p, "ayl", here, here, yl)

    def a3(p):
        left, right = 4 * c + mod4(y - 1), 4 * c + mod4(y + 1)
        arrived(p, "ayr", tok.at[p, left])
        here = tok.at[p, left, pl.ds(0, 2)]
        send(p, "arr", here, here, yr)
        arrived(p, "ayl", tok.at[p, right])
        here = tok.at[p, right, pl.ds(2, 2)]
        send(p, "arl", here, here, yl)

    def a4(p):
        far = 4 * c + mod4(y + 2)
        arrived(p, "arr", tok.at[p, far, pl.ds(0, 2)])
        arrived(p, "arl", tok.at[p, far, pl.ds(2, 2)])
        here = tok.at[p, pl.ds(4 * c, 4)]
        send(p, "ac", here, here, core)

    def m1(p):
        arrived(p, "ac", tok.at[p, pl.ds(4 * (1 - c), 4)])
        if p == 0:
            loads[0].wait()
            loads[1].wait()

        def tile(i, carry):
            columns = pl.ds(pl.multiple_of(i * 256, 256), 256)
            lhs = tok[p].reshape(8 * rows, tok.shape[-1])
            product = jnp.dot(lhs, wgu[:, columns], preferred_element_type=F32)
            part[p, :, :, columns] = product.astype(BF16).reshape(8, rows, 256)
            return carry

        lax.fori_loop(0, 2 * ff // 256, tile, 0)
        send(p, "s1g", part.at[p, two(x + 2), :, g], s1g.at[p], xr)
        send(p, "s1u", part.at[p, two(x + 2), :, u], s1u.at[p], xl)
        send(p, "sug", part.at[p, two(x + 1), :, u], sug.at[p], xr)
        send(p, "sgu", part.at[p, two(x - 1), :, g], sgu.at[p], xl)

    def x2(p):
        arrived(p, "s1g", s1g.at[p])
        part[p, two(x + 1), :, g] = (f32(part[p, two(x + 1), :, g]) + f32(s1g[p])).astype(BF16)
        send(p, "lg", part.at[p, two(x + 1), :, g], lg.at[p], xr)
        arrived(p, "s1u", s1u.at[p])
        part[p, two(x - 1), :, u] = (f32(part[p, two(x - 1), :, u]) + f32(s1u[p])).astype(BF16)
        send(p, "lu", part.at[p, two(x - 1), :, u], lu.at[p], xl)

    def z1(p):
        arrived(p, "lg", lg.at[p])
        arrived(p, "sgu", sgu.at[p])
        arrived(p, "lu", lu.at[p])
        arrived(p, "sug", sug.at[p])

        def total(b, cols, long, short):
            return f32(part[p, 2 * x + b, :, cols]) + f32(long[p, b]) + f32(short[p, b])

        zsend[p, :, g] = total(1 - h, g, lg, sgu).astype(BF16)
        zsend[p, :, u] = total(1 - h, u, lu, sug).astype(BF16)
        send(p, "z", zsend.at[p], zrecv.at[p], zpeer)
        zkeep[p, :, g] = total(h, g, lg, sgu)
        zkeep[p, :, u] = total(h, u, lu, sug)

    def hidden(p):
        arrived(p, "z", zrecv.at[p])
        gate = zkeep[p, :, g] + f32(zrecv[p, :, g])
        up = zkeep[p, :, u] + f32(zrecv[p, :, u])
        mine = 2 * x + h
        hid[p, mine] = (jax.nn.silu(gate) * up).astype(BF16)
        here = hid.at[p, mine]
        send(p, "ez", here, here, zpeer)
        send(p, "eor", here, here, xr)
        send(p, "eol", here, here, xl)

    def e2(p):
        here = hid.at[p, 2 * x + 1 - h]
        arrived(p, "ez", here)
        send(p, "epr", here, here, xr)
        send(p, "epl", here, here, xl)

    def e3(p):
        here = hid.at[p, 2 * mod4(x - 1) + h]
        arrived(p, "eor", here)
        send(p, "err", here, here, xr)
        here = hid.at[p, 2 * mod4(x + 1) + 1 - h]
        arrived(p, "epl", here)
        send(p, "erl", here, here, xl)

    def m2(p):
        arrived(p, "eol", hid.at[p, 2 * mod4(x + 1) + h])
        arrived(p, "epr", hid.at[p, 2 * mod4(x - 1) + 1 - h])
        arrived(p, "err", hid.at[p, 2 * mod4(x + 2) + h])
        arrived(p, "erl", hid.at[p, 2 * mod4(x + 2) + 1 - h])
        if p == 0:
            loads[2].wait()

        def tile(i, carry):
            columns = pl.ds(pl.multiple_of(i * 256, 256), 256)
            lhs = hid[p].reshape(8 * rows, ff)
            product = jnp.dot(lhs, wd[:, columns], preferred_element_type=F32)
            outp[p, :, :, columns] = product.astype(BF16).reshape(8, rows, 256)
            return carry

        lax.fori_loop(0, 2 * mid // 256, tile, 0)
        send(p, "gc", outp.at[p, pl.ds(4 * (1 - c), 4)], crecv.at[p], core)

    def g2(p):
        arrived(p, "gc", crecv.at[p])
        osum[p] = (f32(outp[p, pl.ds(4 * c, 4)]) + f32(crecv[p])).astype(BF16)
        send(p, "y1a", osum.at[p, mod4(y + 2), :, ca], y1a.at[p], yr)
        send(p, "y1b", osum.at[p, mod4(y + 2), :, cb], y1b.at[p], yl)
        send(p, "ysb", osum.at[p, mod4(y + 1), :, cb], ysb.at[p], yr)
        send(p, "ysa", osum.at[p, mod4(y - 1), :, ca], ysa.at[p], yl)

    def g3(p):
        arrived(p, "y1a", y1a.at[p])
        there = mod4(y + 1)
        osum[p, there, :, ca] = (f32(osum[p, there, :, ca]) + f32(y1a[p])).astype(BF16)
        send(p, "yla", osum.at[p, there, :, ca], yla.at[p], yr)
        arrived(p, "y1b", y1b.at[p])
        there = mod4(y - 1)
        osum[p, there, :, cb] = (f32(osum[p, there, :, cb]) + f32(y1b[p])).astype(BF16)
        send(p, "ylb", osum.at[p, there, :, cb], ylb.at[p], yl)

    def g4(p):
        arrived(p, "yla", yla.at[p])
        arrived(p, "ysa", ysa.at[p])
        arrived(p, "ylb", ylb.at[p])
        arrived(p, "ysb", ysb.at[p])
        a = f32(osum[p, y, :, ca]) + f32(yla[p]) + f32(ysa[p])
        b = f32(osum[p, y, :, cb]) + f32(ylb[p]) + f32(ysb[p])
        zos[p, :, :, ca] = a.astype(BF16).reshape(4, r, mid)
        zos[p, :, :, cb] = b.astype(BF16).reshape(4, r, mid)
        for k in (1, 2, 3):
            send(p, "gz%d" % k, zos.at[p, mod4(zl + k)], zor.at[p, k - 1], zs[k])

    def g5(p):
        total = f32(zos[p, zl])
        for k in (1, 2, 3):
            arrived(p, "gz%d" % k, zor.at[p, k - 1])
            total = total + f32(zor[p, k - 1])
        out[pl.ds(p * r, r), :] = total.astype(BF16)

    steps = dict(zip(STEPS, (a1, a2, a3, a4, m1, x2, z1, hidden, e2, e3, m2, g2, g3, g4, g5)))
    for p, step in step_order(panels):
        steps[step](p)
    for copy in sent:
        copy.wait_send()


def shards(tokens, gate_weight, up_weight, down_weight):
    n = PANELS
    r = 64 // n
    rows = 4 * r
    depth, ff = gate_weight.shape
    wide = down_weight.shape[1]
    vmem = pltpu.VMEM
    scratch = [
        vmem((depth, 2 * ff), BF16),
        vmem((ff, wide), BF16),
        vmem((n, 8, 4, r, depth), BF16),
        vmem((n, 8, rows, 2 * ff), BF16),
    ]
    scratch += [vmem((n, 2, rows, ff), BF16)] * 6
    scratch += [
        vmem((n, rows, 2 * ff), BF16),
        vmem((n, rows, 2 * ff), F32),
        vmem((n, rows, 2 * ff), BF16),
        vmem((n, 8, rows, ff), BF16),
        vmem((n, 8, rows, wide), BF16),
        vmem((n, 4, rows, wide), BF16),
        vmem((n, 4, rows, wide), BF16),
    ]
    scratch += [vmem((n, rows, wide // 2), BF16)] * 6
    scratch += [
        vmem((n, 4, r, wide), BF16),
        vmem((n, 3, r, wide), BF16),
        pltpu.SemaphoreType.DMA((n, len(COPIES))),
        pltpu.SemaphoreType.DMA((n, len(COPIES))),
        pltpu.SemaphoreType.DMA((3,)),
    ]
    whole = pl.BlockSpec(memory_space=pltpu.VMEM)
    anywhere = pl.BlockSpec(memory_space=pl.ANY)
    return pl.pallas_call(
        functools.partial(kernel, n),
        out_shape=jax.ShapeDtypeStruct(tokens.shape, BF16),
        in_specs=[whole, anywhere, anywhere, anywhere],
        out_specs=whole,
        scratch_shapes=scratch,
        compiler_params=pltpu.CompilerParams(
            collective_id=0, has_side_effects=True, vmem_limit_bytes=60 << 20
        ),
        name="swiglu",
    )(tokens, gate_weight, up_weight, down_weight)


def solution(mesh):
    return jax.shard_map(
        shards,
        mesh=mesh,
        in_specs=(
            P(("gx", "gy"), "gz"),
            P("gz", ("gx", "gy")),
            P("gz", ("gx", "gy")),
            P(("gx", "gy"), "gz"),
        ),
        out_specs=P(("gx", "gy"), "gz"),
        check_vma=False,
    )
```

time: 839 us -> 156 us (0.19)
  waiting for transfers between devices: 795 us -> 0 us
  Pallas kernels: 0 us -> 155 us
  matrix products: 26.8 us -> 0 us
  between operations: 13.5 us -> 0.01 us
    all_gather x5 -> x0, waiting for transfers between devices: 529 us -> none  [the longest x1 137 us: shards(): lax.all_gather(gate_weight, 'gy', axis=1, tiled=True)]
    reduce_scatter x3 -> x0, waiting for transfers between devices: 263 us -> none  [the longest x1 121 us: shards(): lax.psum_scatter(up_partial.astype(jnp.bfloat16), 'gz', scatter_dimension...]
    pallas_call x0 -> x1, Pallas kernels: none -> 155 us  [shards(): pl.pallas_call(functools.partial(kernel, n), out_shape=jax.ShapeDtypeStru...]
    dot_general x3 -> x0, matrix products: 26.8 us -> none  [the longest x2 17.6 us: column_product(): return jnp.dot(gathered, weight_piece, preferred_element_type=jnp.float32)]
  transfers between devices with their start and end apart: 8 -> 0, of which waited for: 8 -> 0; matrix products, arithmetic and copies ran while one was open for 2% -> 0% of each run, Pallas kernels for 0% -> 0%
where the time goes in v1:
time: 156 us
  Pallas kernels  155 us (99%)
  local copies, waits for them, and re-layouts  1.57 us (1%)
    pallas_call x1, Pallas kernels, shards(): pl.pallas_call(functools.partial(kernel, n), out_shape=jax.ShapeDtypeStru...  155 us

profile of v1, /device:TPU:1, one launch (start us, length us, event | category | flops | bytes accessed | tf_op | source)
XLA Modules:
  0.0 156.1 jit_solution(2850394855926379071)
XLA Ops:
  0.0 154.6 %swiglu.1 = bf16[64,1024]{1,0:T(8,128)(2,1)} custom-call(bf16[64,1024]{1,0:T(8,128)(2,1)} %tokens.1, bf16[1024,896]{1,0:T(8,128)(2,1)} %gate_hbm.1, bf16[1024,896]{1,0:T(8,128)(2,1)} %up_hbm.1, bf16[896,1024]{1,0:T(8,128)(2,1)} %down_hbm.1), custom_call_target="tpu_custom_call" | custom-call | tf_op jit(solution)/shard_map/swiglu/pallas_call | solution.py:327
  154.6 1.6 %copy.6 = bf16[64,1024]{1,0:T(8,128)(2,1)} copy(bf16[64,1024]{1,0:T(8,128)(2,1)} %swiglu.1) | data formatting | bytes 262144

commit v2 on v0

v2 whole, which is shorter than its diff:
```python
import jax
import jax.numpy as jnp
from jax import lax
from jax.experimental import pallas as pl
from jax.experimental.pallas import tpu as pltpu
from jax.sharding import PartitionSpec as P

PANELS = ((0, 0), (1, 0), (3, 0), (2, 0), (1, 1), (3, 1), (2, 1), (0, 1))
BF16, F32 = jnp.bfloat16, jnp.float32
ORDER = (
    ("A2", 0), ("A3", 0), ("A2", 1), ("A4", 0), ("A3", 1), ("A2", 3), ("M1", 0), ("A4", 1),
    ("A3", 3), ("A2", 4), ("A2", 2), ("M1", 1), ("A4", 3), ("X2", 0), ("A2", 6), ("A2", 7),
    ("A3", 4), ("A3", 2), ("M1", 3), ("X2", 1), ("A4", 2), ("A3", 6), ("A2", 5), ("Z1", 0),
    ("M1", 2), ("X2", 3), ("A3", 5), ("A4", 4), ("Z1", 1), ("A4", 5), ("A3", 7), ("A4", 6),
    ("H", 0), ("M1", 4), ("X2", 2), ("Z1", 3), ("M1", 5), ("X2", 4), ("H", 1), ("Z1", 2),
    ("E1", 0), ("X2", 5), ("H", 3), ("A4", 7), ("E2", 0), ("M1", 6), ("Z1", 4), ("M1", 7),
    ("Z1", 5), ("E3", 0), ("H", 2), ("H", 4), ("X2", 6), ("X2", 7), ("H", 5), ("E1", 1),
    ("M2", 0), ("Z1", 6), ("E2", 1), ("E1", 2), ("E2", 2), ("E1", 3), ("E3", 1), ("E2", 3),
    ("Z1", 7), ("E3", 2), ("E1", 4), ("E2", 4), ("H", 6), ("E1", 5), ("G2", 0), ("M2", 1),
    ("E3", 3), ("E2", 5), ("H", 7), ("G2", 1), ("E3", 4), ("E1", 6), ("M2", 2), ("E2", 6),
    ("M2", 3), ("E3", 5), ("E1", 7), ("G2", 2), ("M2", 4), ("E2", 7), ("G4", 1), ("E3", 6),
    ("G2", 3), ("G2", 4), ("M2", 5), ("E3", 7), ("G4", 2), ("M2", 6), ("G2", 5), ("G2", 6),
    ("M2", 7), ("G4", 0), ("G4", 3), ("G4", 4), ("G2", 7), ("G4", 5), ("G4", 6), ("G4", 7),
)
ARRIVALS = ("az", "ay", "ar", "ac", "s1", "lo", "z", "ez", "e1", "e2", "gc", "gy")
SENDS = ("tokens", "sums", "hidden", "outputs")


def kernel(
    tokens, gate_hbm, up_hbm, down_hbm, out,
    wgu, wd, tok, part, first, second, zsend, zkeep, zrecv, hid, outp,
    crecv, osum, ysum, zos, zown, zor, send_sem, recv_sem, last_sem, weight_sem,
):
    gx, gy, gz = lax.axis_index("gx"), lax.axis_index("gy"), lax.axis_index("gz")
    x, h, y, c, zl = lax.rem(gz, 4), gz // 4, gx // 2, lax.rem(gx, 2), gy
    rows = tok.shape[2]
    ff = gate_hbm.shape[1]

    def mod4(v):
        return lax.rem(v + 4, 4)

    def device(x=x, h=h, y=y, c=c, zl=zl):
        return {"gx": 2 * y + c, "gy": zl, "gz": 4 * h + x}

    xr, xl = device(x=mod4(x + 1)), device(x=mod4(x - 1))
    yr, yl, yf = device(y=mod4(y + 1)), device(y=mod4(y - 1)), device(y=mod4(y + 2))
    zpeer = device(h=1 - h)
    core = device(c=1 - c)
    zup = [None] + [device(zl=mod4(zl + k)) for k in (1, 2, 3)]
    zdown = [None, zup[3], zup[2], zup[1]]

    barrier = pltpu.get_barrier_semaphore()
    peers = (xr, xl, yr, yl, yf, zpeer, core, zup[1], zup[2], zup[3])
    for peer in peers:
        pl.semaphore_signal(barrier, inc=1, device_id=peer, device_id_type=pl.DeviceIdType.MESH)
    loads = [
        pltpu.make_async_copy(gate_hbm, wgu.at[:, pl.ds(0, ff)], weight_sem.at[0]),
        pltpu.make_async_copy(up_hbm, wgu.at[:, pl.ds(ff, ff)], weight_sem.at[1]),
        pltpu.make_async_copy(down_hbm, wd, weight_sem.at[2]),
    ]
    for load in loads:
        load.start()
    cy = 4 * c + y
    for p, (offset, q) in enumerate(PANELS):
        if offset == 0:
            tok[p, cy] = tokens[pl.ds(q * rows, rows), :]
    pl.semaphore_wait(barrier, len(peers))

    def send(p, group, name, src, dst, to):
        arrival = recv_sem.at[p, ARRIVALS.index(name)] if name in ARRIVALS else last_sem.at[PANELS[p][1]]
        pltpu.make_async_remote_copy(
            src_ref=src, dst_ref=dst, send_sem=send_sem.at[p, SENDS.index(group)],
            recv_sem=arrival, device_id=to, device_id_type=pl.DeviceIdType.MESH,
        ).start()

    def arrived(p, name, extent):
        arrival = recv_sem.at[p, ARRIVALS.index(name)] if name in ARRIVALS else last_sem.at[p]
        pltpu.make_async_remote_copy(
            src_ref=extent, dst_ref=extent, send_sem=send_sem.at[0, 0],
            recv_sem=arrival, device_id=core, device_id_type=pl.DeviceIdType.MESH,
        ).wait_recv()

    def flush(p):
        blocks = 8 if PANELS[p][0] else 7
        extents = (
            tok.at[p, pl.ds(0, blocks)], part.at[p, pl.ds(0, 7)],
            hid.at[p, pl.ds(0, 7)], outp.at[p, pl.ds(0, blocks)],
        )
        for i, extent in enumerate(extents):
            pltpu.make_async_remote_copy(
                src_ref=extent, dst_ref=extent, send_sem=send_sem.at[p, i],
                recv_sem=recv_sem.at[0, 0], device_id=core, device_id_type=pl.DeviceIdType.MESH,
            ).wait_send()

    g, u = pl.ds(0, ff), pl.ds(ff, ff)

    def two(j):
        return pl.ds(2 * mod4(j), 2)

    def f32(v):
        return v.astype(F32)

    def a1(p):
        offset, q = PANELS[p]
        if offset:
            send(p, "tokens", "az", tokens.at[pl.ds(q * rows, rows)], tok.at[p, cy], zdown[offset])

    def a2(p):
        here = tok.at[p, cy]
        if PANELS[p][0]:
            arrived(p, "az", here)
        send(p, "tokens", "ay", here, here, yr)
        send(p, "tokens", "ay", here, here, yl)

    def a3(p):
        arrived(p, "ay", tok.at[p, pl.ds(0, 2)])
        here = tok.at[p, 4 * c + mod4(y - 1), pl.ds(0, rows // 2)]
        send(p, "tokens", "ar", here, here, yr)
        here = tok.at[p, 4 * c + mod4(y + 1), pl.ds(rows // 2, rows // 2)]
        send(p, "tokens", "ar", here, here, yl)

    def a4(p):
        arrived(p, "ar", tok.at[p, 0])
        here = tok.at[p, pl.ds(4 * c, 4)]
        send(p, "tokens", "ac", here, here, core)

    def m1(p):
        arrived(p, "ac", tok.at[p, pl.ds(0, 4)])
        if p == 0:
            loads[0].wait()
            loads[1].wait()

        def tile(i, carry):
            columns = pl.ds(pl.multiple_of(i * 256, 256), 256)
            lhs = tok[p].reshape(8 * rows, tok.shape[-1])
            product = jnp.dot(lhs, wgu[:, columns], preferred_element_type=F32)
            part[p, :, :, columns] = product.astype(BF16).reshape(8, rows, 256)
            return carry

        tiles = 2 * ff // 256
        lax.fori_loop(0, (tiles + 1) // 2, tile, 0)
        send(p, "sums", "s1", part.at[p, two(x + 2), :, g], first.at[p, 0], xr)
        send(p, "sums", "lo", part.at[p, two(x - 1), :, g], second.at[p, 1], xl)
        lax.fori_loop((tiles + 1) // 2, tiles, tile, 0)
        send(p, "sums", "s1", part.at[p, two(x + 2), :, u], first.at[p, 1], xl)
        send(p, "sums", "lo", part.at[p, two(x + 1), :, u], second.at[p, 3], xr)

    def x2(p):
        arrived(p, "s1", first.at[p])
        there = two(x + 1)
        part[p, there, :, g] = (f32(part[p, there, :, g]) + f32(first[p, 0])).astype(BF16)
        send(p, "sums", "lo", part.at[p, there, :, g], second.at[p, 0], xr)
        there = two(x - 1)
        part[p, there, :, u] = (f32(part[p, there, :, u]) + f32(first[p, 1])).astype(BF16)
        send(p, "sums", "lo", part.at[p, there, :, u], second.at[p, 2], xl)

    def z1(p):
        arrived(p, "lo", second.at[p])

        def total(b, cols, i):
            return f32(part[p, 2 * x + b, :, cols]) + f32(second[p, i, b]) + f32(second[p, i + 1, b])

        zsend[p, :, g] = total(1 - h, g, 0).astype(BF16)
        zsend[p, :, u] = total(1 - h, u, 2).astype(BF16)
        send(p, "sums", "z", zsend.at[p], zrecv.at[p], zpeer)
        zkeep[p, :, g] = total(h, g, 0)
        zkeep[p, :, u] = total(h, u, 2)

    def hidden(p):
        arrived(p, "z", zrecv.at[p])
        gate = zkeep[p, :, g] + f32(zrecv[p, :, g])
        up = zkeep[p, :, u] + f32(zrecv[p, :, u])
        mine = 2 * x + h
        hid[p, mine] = (jax.nn.silu(gate) * up).astype(BF16)
        here = hid.at[p, mine]
        send(p, "hidden", "ez", here, here, zpeer)

    def e1(p):
        here = hid.at[p, 2 * x + h]
        send(p, "hidden", "e1", here, here, xr)
        send(p, "hidden", "e2", here, here, xl)

    def e2(p):
        here = hid.at[p, 2 * x + 1 - h]
        arrived(p, "ez", here)
        send(p, "hidden", "e1", here, here, xl)
        send(p, "hidden", "e2", here, here, xr)

    def e3(p):
        arrived(p, "e1", hid.at[p, pl.ds(0, 2)])
        here = hid.at[p, 2 * mod4(x - 1) + h]
        send(p, "hidden", "e2", here, here, xr)
        here = hid.at[p, 2 * mod4(x + 1) + 1 - h]
        send(p, "hidden", "e2", here, here, xl)

    def m2(p):
        arrived(p, "e2", hid.at[p, pl.ds(0, 4)])
        if p == 0:
            loads[2].wait()

        def tile(i, carry):
            columns = pl.ds(pl.multiple_of(i * 256, 256), 256)
            lhs = hid[p].reshape(8 * rows, ff)
            product = jnp.dot(lhs, wd[:, columns], preferred_element_type=F32)
            outp[p, :, :, columns] = product.astype(BF16).reshape(8, rows, 256)
            return carry

        lax.fori_loop(0, wd.shape[1] // 256, tile, 0)
        send(p, "outputs", "gc", outp.at[p, pl.ds(4 * (1 - c), 4)], crecv.at[p], core)

    def g2(p):
        if p == len(PANELS) - 1:
            g5(0)
        arrived(p, "gc", crecv.at[p])
        osum[p] = (f32(outp[p, pl.ds(4 * c, 4)]) + f32(crecv[p])).astype(BF16)
        send(p, "outputs", "gy", osum.at[p, mod4(y + 2)], ysum.at[p, 1], yf)
        send(p, "outputs", "gy", osum.at[p, mod4(y + 1)], ysum.at[p, 0], yr)
        send(p, "outputs", "gy", osum.at[p, mod4(y - 1)], ysum.at[p, 2], yl)

    def g4(p):
        offset, q = PANELS[p]
        arrived(p, "gy", ysum.at[p])
        total = f32(osum[p, y]) + f32(ysum[p, 0]) + f32(ysum[p, 1]) + f32(ysum[p, 2])
        if offset == 0:
            zown[q] = total
        else:
            zos[p] = total.astype(BF16)
            send(p, "outputs", "gz", zos.at[p], zor.at[q, offset - 1], zup[offset])

    def g5(q):
        arrived(q, "last", zor.at[q])
        total = zown[q] + f32(zor[q, 0]) + f32(zor[q, 1]) + f32(zor[q, 2])
        out[pl.ds(q * rows, rows), :] = total.astype(BF16)

    steps = dict(
        A2=a2, A3=a3, A4=a4, M1=m1, X2=x2, Z1=z1, H=hidden, E1=e1, E2=e2, E3=e3, M2=m2, G2=g2, G4=g4
    )
    steps[ORDER[0][0]](ORDER[0][1])
    for p in range(len(PANELS)):
        a1(p)
    for step, p in ORDER[1:]:
        steps[step](p)
    g5(1)
    for p in range(len(PANELS)):
        flush(p)


def shards(tokens, gate_weight, up_weight, down_weight):
    n = len(PANELS)
    rows = tokens.shape[0] // 2
    depth, ff = gate_weight.shape
    wide = down_weight.shape[1]
    vmem = pltpu.VMEM
    scratch = [
        vmem((depth, 2 * ff), BF16),
        vmem((ff, wide), BF16),
        vmem((n, 8, rows, depth), BF16),
        vmem((n, 8, rows, 2 * ff), BF16),
    ]
    scratch += [
        vmem((n, 2, 2, rows, ff), BF16),
        vmem((n, 4, 2, rows, ff), BF16),
        vmem((n, rows, 2 * ff), BF16),
        vmem((n, rows, 2 * ff), F32),
        vmem((n, rows, 2 * ff), BF16),
        vmem((n, 8, rows, ff), BF16),
        vmem((n, 8, rows, wide), BF16),
        vmem((n, 4, rows, wide), BF16),
        vmem((n, 4, rows, wide), BF16),
    ]
    scratch += [
        vmem((n, 3, rows, wide), BF16),
        vmem((n, rows, wide), BF16),
        vmem((2, rows, wide), F32),
        vmem((2, 3, rows, wide), BF16),
        pltpu.SemaphoreType.DMA((n, len(SENDS))),
        pltpu.SemaphoreType.DMA((n, len(ARRIVALS))),
        pltpu.SemaphoreType.DMA((2,)),
        pltpu.SemaphoreType.DMA((3,)),
    ]
    whole = pl.BlockSpec(memory_space=pltpu.VMEM)
    anywhere = pl.BlockSpec(memory_space=pl.ANY)
    return pl.pallas_call(
        kernel,
        out_shape=jax.ShapeDtypeStruct(tokens.shape, BF16),
        in_specs=[whole, anywhere, anywhere, anywhere],
        out_specs=whole,
        scratch_shapes=scratch,
        compiler_params=pltpu.CompilerParams(
            collective_id=0, has_side_effects=True, vmem_limit_bytes=60 << 20
        ),
        name="swiglu",
    )(tokens, gate_weight, up_weight, down_weight)


def solution(mesh):
    return jax.shard_map(
        shards,
        mesh=mesh,
        in_specs=(
            P(("gx", "gy"), "gz"),
            P("gz", ("gx", "gy")),
            P("gz", ("gx", "gy")),
            P(("gx", "gy"), "gz"),
        ),
        out_specs=P(("gx", "gy"), "gz"),
        check_vma=False,
    )
```

time: 839 us -> 129 us (0.15)
  waiting for transfers between devices: 795 us -> 0 us
  Pallas kernels: 0 us -> 127 us
  matrix products: 26.8 us -> 0 us
  between operations: 13.5 us -> 0.01 us
    all_gather x5 -> x0, waiting for transfers between devices: 529 us -> none  [the longest x1 137 us: shards(): lax.all_gather(gate_weight, 'gy', axis=1, tiled=True)]
    reduce_scatter x3 -> x0, waiting for transfers between devices: 263 us -> none  [the longest x1 121 us: shards(): lax.psum_scatter(up_partial.astype(jnp.bfloat16), 'gz', scatter_dimension...]
    pallas_call x0 -> x1, Pallas kernels: none -> 127 us  [shards(): pl.pallas_call(kernel, out_shape=jax.ShapeDtypeStruct(tokens.shape, BF16)...]
    dot_general x3 -> x0, matrix products: 26.8 us -> none  [the longest x2 17.6 us: column_product(): return jnp.dot(gathered, weight_piece, preferred_element_type=jnp.float32)]
  transfers between devices with their start and end apart: 8 -> 0, of which waited for: 8 -> 0; matrix products, arithmetic and copies ran while one was open for 2% -> 0% of each run, Pallas kernels for 0% -> 0%
where the time goes in v2:
time: 129 us; the launch traced here: 128 us
  Pallas kernels  127 us (98%)
  local copies, waits for them, and re-layouts  1.57 us (1%)
    pallas_call x1, Pallas kernels, shards(): pl.pallas_call(kernel, out_shape=jax.ShapeDtypeStruct(tokens.shape, BF16)...  127 us

profile of v2, /device:TPU:1, one launch (start us, length us, event | category | flops | bytes accessed | tf_op | source)
XLA Modules:
  0.0 128.5 jit_solution(217974922108027045)
XLA Ops:
  0.0 126.9 %swiglu.1 = bf16[64,1024]{1,0:T(8,128)(2,1)} custom-call(bf16[64,1024]{1,0:T(8,128)(2,1)} %tokens.1, bf16[1024,896]{1,0:T(8,128)(2,1)} %gate_hbm.1, bf16[1024,896]{1,0:T(8,128)(2,1)} %up_hbm.1, bf16[896,1024]{1,0:T(8,128)(2,1)} %down_hbm.1), custom_call_target="tpu_custom_call" | custom-call | tf_op jit(solution)/shard_map/swiglu/pallas_call | solution.py:283
  126.9 1.6 %copy.6 = bf16[64,1024]{1,0:T(8,128)(2,1)} copy(bf16[64,1024]{1,0:T(8,128)(2,1)} %swiglu.1) | data formatting | bytes 262144

commit v3 on v0

v3 whole, which is shorter than its diff:
```python
import jax
import jax.numpy as jnp
from jax import lax
from jax.experimental import pallas as pl
from jax.experimental.pallas import tpu as pltpu
from jax.sharding import PartitionSpec as P

NEAR, MIDDLE, OWN = 0, 1, 10
SHIFTED = {
    2: (1, 0, 32), 3: (3, 0, 32), 4: (2, 0, 32), 5: (1, 32, 32),
    6: (3, 32, 16), 7: (3, 48, 16), 8: (2, 32, 16), 9: (2, 48, 16),
}
PANELS = 11
BIG, SMALL = (1, 2, 3, 4, 5), (0, 6, 7, 8, 9, 10)
BF16, F32 = jnp.bfloat16, jnp.float32
ORDER = (
    ("A2", 0), ("A2", 1), ("A2", 10), ("A4", 10), ("M1", 10), ("A4", 0), ("A2", 2), ("M1", 0),
    ("A4", 1), ("X2", 10), ("A2", 3), ("M1", 1), ("X2", 0), ("A2", 6), ("A2", 4), ("A4", 2),
    ("A2", 5), ("A4", 3), ("M1", 2), ("A4", 6), ("Z1", 10), ("X2", 1), ("A2", 7), ("A2", 9),
    ("A2", 8), ("Z1", 0), ("M1", 3), ("H", 0), ("A4", 4), ("A4", 7), ("A4", 9), ("A4", 5),
    ("X2", 2), ("Z1", 1), ("M1", 6), ("X2", 3), ("Z1", 2), ("M1", 7), ("H", 1), ("X2", 6),
    ("M1", 4), ("X2", 7), ("Z1", 3), ("M1", 5), ("Z1", 6), ("Z1", 7), ("X2", 4), ("A4", 8),
    ("H", 3), ("E1", 1), ("E2", 1), ("H", 2), ("X2", 5), ("M1", 8), ("Z1", 4), ("E3", 1),
    ("M1", 9), ("Z1", 5), ("E1", 3), ("X2", 8), ("H", 7), ("M2", 1), ("H", 4), ("E1", 2),
    ("E2", 2), ("E2", 3), ("X2", 9), ("Z1", 8), ("E1", 7), ("E3", 2), ("G2", 1), ("E1", 4),
    ("H", 5), ("E3", 3), ("E2", 7), ("E2", 4), ("Z1", 9), ("H", 6), ("M2", 2), ("E1", 5),
    ("H", 8), ("E2", 5), ("M2", 3), ("E3", 7), ("E3", 4), ("G2", 2), ("G4", 1), ("H", 9),
    ("E1", 6), ("E2", 6), ("H", 10), ("G2", 3), ("E3", 5), ("E1", 8), ("M2", 7), ("E2", 8),
    ("M2", 4), ("E3", 6), ("E1", 9), ("E2", 9), ("E1", 0), ("G2", 7), ("M2", 5), ("G2", 4),
    ("E3", 8), ("G4", 2), ("E2", 0), ("M2", 6), ("E3", 9), ("E1", 10), ("E2", 10), ("G2", 5),
    ("M2", 8), ("E3", 0), ("G2", 6), ("M2", 9), ("E3", 10), ("G4", 7), ("G2", 8), ("G4", 4),
    ("M2", 0), ("G2", 9), ("G4", 3), ("G4", 5), ("G4", 6), ("G2", 0), ("G4", 8), ("G4", 9),
    ("M2", 10), ("G2", 10), ("G4", 10), ("G4", 0),
)
FIRST_UP = next(p for step, p in ORDER if step == "M1")
FIRST_DOWN = next(p for step, p in ORDER if step == "M2")
ARRIVALS = ("az", "ay", "ac", "s1", "lo", "z", "ez", "e1", "e2", "gc", "gy")
SENDS = ("tokens", "sums", "hidden", "outputs")
BUFFERS = (
    "tok", "part", "first", "second", "zsend", "zkeep", "zrecv", "hid", "outp", "crecv", "osum", "ysum", "zos"
)


def buffers(panels, tall, depth, ff, wide):
    rows = tall[0] * tall[-1] if len(tall) > 1 else tall[0]
    shapes = (
        (8,) + tall + (depth,), (8, rows, 2 * ff), (2, 2, rows, ff), (4, 2, rows, ff), (rows, 2 * ff),
        (rows, 2 * ff), (rows, 2 * ff), (8, rows, ff), (8, rows, wide), (4, rows, wide),
        (4, rows, wide), (4, rows, wide), (rows, wide),
    )
    return [
        pltpu.VMEM((panels,) + shape, F32 if name == "zkeep" else BF16)
        for name, shape in zip(BUFFERS, shapes)
    ]


def kernel(tokens_hbm, gate_hbm, up_hbm, down_hbm, out, tokens, wgu, wd, total, zor, *scratch):
    big = dict(zip(BUFFERS, scratch))
    small = dict(zip(BUFFERS, scratch[len(BUFFERS):]))
    send_sem, recv_sem, last_sem, weight_sem = scratch[2 * len(BUFFERS):]
    gx, gy, gz = lax.axis_index("gx"), lax.axis_index("gy"), lax.axis_index("gz")
    x, h, y, c, zl = lax.rem(gz, 4), gz // 4, gx // 2, lax.rem(gx, 2), gy
    ff = gate_hbm.shape[1]

    def panel(p, name):
        group, members = (big, BIG) if p in BIG else (small, SMALL)
        return group[name].at[members.index(p)]

    def mod4(v):
        return lax.rem(v + 4, 4)

    def device(x=x, h=h, y=y, c=c, zl=zl):
        return {"gx": 2 * y + c, "gy": zl, "gz": 4 * h + x}

    xr, xl = device(x=mod4(x + 1)), device(x=mod4(x - 1))
    yr, yl, yf = device(y=mod4(y + 1)), device(y=mod4(y - 1)), device(y=mod4(y + 2))
    zpeer = device(h=1 - h)
    core = device(c=1 - c)
    zup = [None] + [device(zl=mod4(zl + k)) for k in (1, 2, 3)]
    zdown = [None, zup[3], zup[2], zup[1]]

    loads = [
        pltpu.make_async_copy(tokens_hbm, tokens, weight_sem.at[3]),
        pltpu.make_async_copy(gate_hbm, wgu.at[:, pl.ds(0, ff)], weight_sem.at[0]),
        pltpu.make_async_copy(up_hbm, wgu.at[:, pl.ds(ff, ff)], weight_sem.at[1]),
        pltpu.make_async_copy(down_hbm, wd, weight_sem.at[2]),
    ]
    barrier = pltpu.get_barrier_semaphore()
    peers = (xr, xl, yr, yl, yf, zpeer, core, zup[1], zup[2], zup[3])
    for peer in peers:
        pl.semaphore_signal(barrier, inc=1, device_id=peer, device_id_type=pl.DeviceIdType.MESH)
    for load in loads:
        load.start()
    cy = 4 * c + y
    total[...] = jnp.zeros_like(total)
    loads[0].wait()
    pl.semaphore_wait(barrier, len(peers))

    def arrival(p, name):
        return recv_sem.at[p, ARRIVALS.index(name)] if name in ARRIVALS else last_sem.at[p]

    def send(p, group, name, src, dst, to):
        pltpu.make_async_remote_copy(
            src_ref=src, dst_ref=dst, send_sem=send_sem.at[2 if p == OWN else int(p in SMALL), SENDS.index(group)],
            recv_sem=arrival(SHIFTED[p][1] // 32 if name == "last" else p, name),
            device_id=to, device_id_type=pl.DeviceIdType.MESH,
        ).start()

    def arrived(p, name, extent):
        pltpu.make_async_remote_copy(
            src_ref=extent, dst_ref=extent, send_sem=send_sem.at[0, 0],
            recv_sem=arrival(p, name), device_id=core, device_id_type=pl.DeviceIdType.MESH,
        ).wait_recv()

    def flush():
        for i, name in enumerate(("tok", "part", "hid", "outp")):
            whole = name in ("tok", "outp")
            blocks = pl.ds(0, 8 if whole else 7)
            extents = (
                big[name].at[:, blocks], small[name].at[pl.ds(0, 5), blocks],
                small[name].at[5, pl.ds(0, 4 if whole else 7)],
            )
            for k, extent in enumerate(extents):
                pltpu.make_async_remote_copy(
                    src_ref=extent, dst_ref=extent, send_sem=send_sem.at[k, i],
                    recv_sem=recv_sem.at[0, 0], device_id=core, device_id_type=pl.DeviceIdType.MESH,
                ).wait_send()

    g, u = pl.ds(0, ff), pl.ds(ff, ff)

    def two(j):
        return pl.ds(2 * mod4(j), 2)

    def f32(v):
        return v.astype(F32)

    upper, lower = pl.ds(0, 2), pl.ds(2, 2)

    def a1(p):
        offset, row, rows = SHIFTED[p]
        source = tokens.at[pl.ds(row // 16, 2)] if rows == 32 else tokens.at[row // 16]
        send(p, "tokens", "az", source, panel(p, "tok").at[cy], zdown[offset])

    def a2(p):
        tok = panel(p, "tok")
        if p == OWN:
            tok[pl.ds(4 * c, 4)] = tokens[...]
        elif p == NEAR:
            send(p, "tokens", "ay", tokens.at[upper], tok.at[pl.ds(4 * c + 2, 2)], yr)
            send(p, "tokens", "ay", tokens.at[upper], tok.at[pl.ds(4 * c, 2)], yl)
        elif p == MIDDLE:
            send(p, "tokens", "ay", tokens.at[lower], tok.at[4 * c + 1], yr)
            send(p, "tokens", "ay", tokens.at[lower], tok.at[4 * c], yl)
            send(p, "tokens", "ay", tokens.at[upper], tok.at[4 * c + 2], yf)
            send(p, "tokens", "ay", tokens.at[lower], tok.at[4 * c + 3], yf)
        else:
            here = tok.at[cy]
            arrived(p, "az", here)
            send(p, "tokens", "ay", here, here, yf)
            send(p, "tokens", "ay", here, here, yr)
            send(p, "tokens", "ay", here, here, yl)

    def a4(p):
        tok = panel(p, "tok")
        if p != OWN:
            arrived(p, "ay", tok.at[pl.ds(0, 3 if p in SHIFTED else 4)])
        here = tok.at[pl.ds(4 * c, 4)]
        send(p, "tokens", "ac", here, here, core)

    def m1(p):
        tok, part, first, second = (panel(p, n) for n in ("tok", "part", "first", "second"))
        arrived(p, "ac", tok.at[pl.ds(0, 4)])
        if p == FIRST_UP:
            loads[1].wait()
            loads[2].wait()
        rows = part.shape[1]

        def tile(i, carry):
            columns = pl.ds(pl.multiple_of(i * 256, 256), 256)
            lhs = tok[...].reshape(8 * rows, tok.shape[-1])
            product = jnp.dot(lhs, wgu[:, columns], preferred_element_type=F32)
            part[:, :, columns] = product.astype(BF16).reshape(8, rows, 256)
            return carry

        tiles = 2 * ff // 256
        lax.fori_loop(0, (tiles + 1) // 2, tile, 0)
        send(p, "sums", "s1", part.at[two(x + 2), :, g], first.at[0], xr)
        send(p, "sums", "lo", part.at[two(x - 1), :, g], second.at[1], xl)
        lax.fori_loop((tiles + 1) // 2, tiles, tile, 0)
        send(p, "sums", "s1", part.at[two(x + 2), :, u], first.at[1], xl)
        send(p, "sums", "lo", part.at[two(x + 1), :, u], second.at[3], xr)

    def x2(p):
        part, first, second = (panel(p, n) for n in ("part", "first", "second"))
        arrived(p, "s1", first)
        there = two(x + 1)
        part[there, :, g] = (f32(part[there, :, g]) + f32(first[0])).astype(BF16)
        send(p, "sums", "lo", part.at[there, :, g], second.at[0], xr)
        there = two(x - 1)
        part[there, :, u] = (f32(part[there, :, u]) + f32(first[1])).astype(BF16)
        send(p, "sums", "lo", part.at[there, :, u], second.at[2], xl)

    def z1(p):
        part, second = panel(p, "part"), panel(p, "second")
        zsend, zkeep, zrecv = (panel(p, n) for n in ("zsend", "zkeep", "zrecv"))
        arrived(p, "lo", second)

        def summed(b, cols, i):
            return f32(part[2 * x + b, :, cols]) + f32(second[i, b]) + f32(second[i + 1, b])

        zsend[:, g] = summed(1 - h, g, 0).astype(BF16)
        zsend[:, u] = summed(1 - h, u, 2).astype(BF16)
        send(p, "sums", "z", zsend, zrecv, zpeer)
        zkeep[:, g] = summed(h, g, 0)
        zkeep[:, u] = summed(h, u, 2)

    def hidden(p):
        hid, zkeep, zrecv = (panel(p, n) for n in ("hid", "zkeep", "zrecv"))
        arrived(p, "z", zrecv)
        gate = zkeep[:, g] + f32(zrecv[:, g])
        up = zkeep[:, u] + f32(zrecv[:, u])
        mine = 2 * x + h
        hid[mine] = (jax.nn.silu(gate) * up).astype(BF16)
        send(p, "hidden", "ez", hid.at[mine], hid.at[mine], zpeer)

    def e1(p):
        here = panel(p, "hid").at[2 * x + h]
        send(p, "hidden", "e1", here, here, xr)
        send(p, "hidden", "e2", here, here, xl)

    def e2(p):
        here = panel(p, "hid").at[2 * x + 1 - h]
        arrived(p, "ez", here)
        send(p, "hidden", "e1", here, here, xl)
        send(p, "hidden", "e2", here, here, xr)

    def e3(p):
        hid = panel(p, "hid")
        arrived(p, "e1", hid.at[pl.ds(0, 2)])
        here = hid.at[2 * mod4(x - 1) + h]
        send(p, "hidden", "e2", here, here, xr)
        here = hid.at[2 * mod4(x + 1) + 1 - h]
        send(p, "hidden", "e2", here, here, xl)

    def m2(p):
        hid, outp, crecv = (panel(p, n) for n in ("hid", "outp", "crecv"))
        arrived(p, "e2", hid.at[pl.ds(0, 4)])
        if p == FIRST_DOWN:
            loads[3].wait()
        rows = hid.shape[1]

        def tile(i, carry):
            columns = pl.ds(pl.multiple_of(i * 256, 256), 256)
            lhs = hid[...].reshape(8 * rows, ff)
            product = jnp.dot(lhs, wd[:, columns], preferred_element_type=F32)
            outp[:, :, columns] = product.astype(BF16).reshape(8, rows, 256)
            return carry

        lax.fori_loop(0, wd.shape[1] // 256, tile, 0)
        send(p, "outputs", "gc", outp.at[pl.ds(4 * (1 - c), 4)], crecv, core)

    def g2(p):
        outp, crecv, osum, ysum = (panel(p, n) for n in ("outp", "crecv", "osum", "ysum"))
        arrived(p, "gc", crecv)
        both = f32(outp[pl.ds(4 * c, 4)]) + f32(crecv[...])
        if p == OWN:
            total[...] += both.reshape(total.shape)
            return
        osum[...] = both.astype(BF16)
        if p == NEAR:
            send(p, "outputs", "gy", osum.at[upper], ysum.at[upper], yr)
            send(p, "outputs", "gy", osum.at[lower], ysum.at[lower], yl)
        elif p == MIDDLE:
            send(p, "outputs", "gy", osum.at[lower], ysum.at[lower], yf)
            send(p, "outputs", "gy", osum.at[0], ysum.at[0], yr)
            send(p, "outputs", "gy", osum.at[1], ysum.at[1], yl)
        else:
            send(p, "outputs", "gy", osum.at[mod4(y + 2)], ysum.at[1], yf)
            send(p, "outputs", "gy", osum.at[mod4(y + 1)], ysum.at[0], yr)
            send(p, "outputs", "gy", osum.at[mod4(y - 1)], ysum.at[2], yl)

    def g4(p):
        osum, ysum, zos = (panel(p, n) for n in ("osum", "ysum", "zos"))
        if p == NEAR:
            arrived(p, "gy", ysum)
            total[pl.ds(0, 32)] += (f32(ysum[upper]) + f32(ysum[lower])).reshape(32, total.shape[1])
        elif p == MIDDLE:
            arrived(p, "gy", ysum)
            total[pl.ds(0, 32)] += f32(ysum[2])
            total[pl.ds(32, 32)] += f32(ysum[0]) + f32(ysum[1]) + f32(ysum[3])
        elif p in SHIFTED:
            offset, row, rows = SHIFTED[p]
            arrived(p, "gy", ysum.at[pl.ds(0, 3)])
            zos[...] = (f32(osum[y]) + f32(ysum[0]) + f32(ysum[1]) + f32(ysum[2])).astype(BF16)
            there = zor.at[row // 32, offset - 1, pl.ds(row % 32, rows)]
            send(p, "outputs", "last", zos, there, zup[offset])

    def g5(q):
        arrived(q, "last", zor.at[q])
        rows = pl.ds(32 * q, 32)
        whole = total[rows] + f32(zor[q, 0]) + f32(zor[q, 1]) + f32(zor[q, 2])
        out[rows, :] = whole.astype(BF16)

    steps = dict(A2=a2, A4=a4, M1=m1, X2=x2, Z1=z1, H=hidden, E1=e1, E2=e2, E3=e3, M2=m2, G2=g2, G4=g4)
    steps[ORDER[0][0]](ORDER[0][1])
    for p in SHIFTED:
        a1(p)
    for step, p in ORDER[1:]:
        steps[step](p)
    g5(0)
    g5(1)
    flush()


def shards(tokens, gate_weight, up_weight, down_weight):
    depth, ff = gate_weight.shape
    quarters = tokens.reshape(4, 16, depth)
    wide = down_weight.shape[1]
    scratch = [
        pltpu.VMEM(quarters.shape, BF16),
        pltpu.VMEM((depth, 2 * ff), BF16),
        pltpu.VMEM((ff, wide), BF16),
        pltpu.VMEM(tokens.shape, F32),
        pltpu.VMEM((2, 3, 32, wide), BF16),
    ]
    scratch += buffers(len(BIG), (2, 16), depth, ff, wide) + buffers(len(SMALL), (16,), depth, ff, wide)
    scratch += [
        pltpu.SemaphoreType.DMA((3, len(SENDS))),
        pltpu.SemaphoreType.DMA((PANELS, len(ARRIVALS))),
        pltpu.SemaphoreType.DMA((2,)),
        pltpu.SemaphoreType.DMA((4,)),
    ]
    whole = pl.BlockSpec(memory_space=pltpu.VMEM)
    anywhere = pl.BlockSpec(memory_space=pl.ANY)
    return pl.pallas_call(
        kernel,
        out_shape=jax.ShapeDtypeStruct(tokens.shape, BF16),
        in_specs=[anywhere] * 4,
        out_specs=whole,
        scratch_shapes=scratch,
        compiler_params=pltpu.CompilerParams(
            collective_id=0, has_side_effects=True, vmem_limit_bytes=60 << 20
        ),
        name="swiglu",
    )(quarters, gate_weight, up_weight, down_weight)


def solution(mesh):
    return jax.shard_map(
        shards,
        mesh=mesh,
        in_specs=(
            P(("gx", "gy"), "gz"),
            P("gz", ("gx", "gy")),
            P("gz", ("gx", "gy")),
            P(("gx", "gy"), "gz"),
        ),
        out_specs=P(("gx", "gy"), "gz"),
        check_vma=False,
    )
```

time: 839 us -> 121 us (0.14)
  waiting for transfers between devices: 795 us -> 0 us
  Pallas kernels: 0 us -> 120 us
  matrix products: 26.8 us -> 0 us
  between operations: 13.5 us -> 0.01 us
    all_gather x5 -> x0, waiting for transfers between devices: 529 us -> none  [the longest x1 137 us: shards(): lax.all_gather(gate_weight, 'gy', axis=1, tiled=True)]
    reduce_scatter x3 -> x0, waiting for transfers between devices: 263 us -> none  [the longest x1 121 us: shards(): lax.psum_scatter(up_partial.astype(jnp.bfloat16), 'gz', scatter_dimension...]
    pallas_call x0 -> x1, Pallas kernels: none -> 120 us  [shards(): pl.pallas_call(kernel, out_shape=jax.ShapeDtypeStruct(tokens.shape, BF16)...]
    dot_general x3 -> x0, matrix products: 26.8 us -> none  [the longest x2 17.6 us: column_product(): return jnp.dot(gathered, weight_piece, preferred_element_type=jnp.float32)]
  transfers between devices with their start and end apart: 8 -> 0, of which waited for: 8 -> 0; matrix products, arithmetic and copies ran while one was open for 2% -> 0% of each run, Pallas kernels for 0% -> 0%
where the time goes in v3:
time: 121 us
  Pallas kernels  120 us (99%)
  local copies, waits for them, and re-layouts  1.57 us (1%)
    pallas_call x1, Pallas kernels, shards(): pl.pallas_call(kernel, out_shape=jax.ShapeDtypeStruct(tokens.shape, BF16)...  120 us

profile of v3, /device:TPU:1, one launch (start us, length us, event | category | flops | bytes accessed | tf_op | source)
XLA Modules:
  0.0 121.2 jit_solution(2116540449190735303)
XLA Ops:
  0.0 119.6 %swiglu.1 = bf16[64,1024]{1,0:T(8,128)(2,1)} custom-call(bf16[4,16,1024]{2,1,0:T(8,128)(2,1)} %bitcast.1, bf16[1024,896]{1,0:T(8,128)(2,1)} %gate_hbm.1, bf16[1024,896]{1,0:T(8,128)(2,1)} %up_hbm.1, bf16[896,1024]{1,0:T(8,128)(2,1)} %down_hbm.1), custom_call_target="tpu_custom_call" | custom-call | tf_op jit(solution)/shard_map/swiglu/pallas_call | solution.py:335
  119.7 1.6 %copy.6 = bf16[64,1024]{1,0:T(8,128)(2,1)} copy(bf16[64,1024]{1,0:T(8,128)(2,1)} %swiglu.1) | data formatting | bytes 262144

commit v4 on v3

--- a/solution.py
+++ b/solution.py
@@ -5,37 +5,54 @@
 from jax.experimental.pallas import tpu as pltpu
 from jax.sharding import PartitionSpec as P
 
-NEAR, MIDDLE, OWN = 0, 1, 10
-SHIFTED = {
-    2: (1, 0, 32), 3: (3, 0, 32), 4: (2, 0, 32), 5: (1, 32, 32),
-    6: (3, 32, 16), 7: (3, 48, 16), 8: (2, 32, 16), 9: (2, 48, 16),
-}
-PANELS = 11
-BIG, SMALL = (1, 2, 3, 4, 5), (0, 6, 7, 8, 9, 10)
+NEAR, FAR, HERE, SHIFTED = range(4)
+PANELS = (
+    (NEAR, 0, 0, 16), (NEAR, 0, 32, 16), (FAR, 0, 0, 16),
+    (SHIFTED, 1, 0, 32), (SHIFTED, 3, 0, 32), (SHIFTED, 2, 0, 16),
+    (SHIFTED, 2, 16, 16), (SHIFTED, 1, 32, 16), (SHIFTED, 1, 48, 16),
+    (SHIFTED, 3, 32, 16), (SHIFTED, 3, 48, 16), (SHIFTED, 2, 32, 16),
+    (SHIFTED, 2, 48, 16), (HERE, 0, 0, 16),
+)
+KIND = tuple(panel[0] for panel in PANELS)
+OWN = KIND.index(HERE)
+BIG = tuple(p for p, panel in enumerate(PANELS) if panel[3] == 32)
+SMALL = tuple(p for p, panel in enumerate(PANELS) if panel[3] == 16 and p != OWN) + (OWN,)
 BF16, F32 = jnp.bfloat16, jnp.float32
+A2, A4, M1, X2, Z1, H, E1, E2, E3, M2, G2, G4 = range(12)
 ORDER = (
-    ("A2", 0), ("A2", 1), ("A2", 10), ("A4", 10), ("M1", 10), ("A4", 0), ("A2", 2), ("M1", 0),
-    ("A4", 1), ("X2", 10), ("A2", 3), ("M1", 1), ("X2", 0), ("A2", 6), ("A2", 4), ("A4", 2),
-    ("A2", 5), ("A4", 3), ("M1", 2), ("A4", 6), ("Z1", 10), ("X2", 1), ("A2", 7), ("A2", 9),
-    ("A2", 8), ("Z1", 0), ("M1", 3), ("H", 0), ("A4", 4), ("A4", 7), ("A4", 9), ("A4", 5),
-    ("X2", 2), ("Z1", 1), ("M1", 6), ("X2", 3), ("Z1", 2), ("M1", 7), ("H", 1), ("X2", 6),
-    ("M1", 4), ("X2", 7), ("Z1", 3), ("M1", 5), ("Z1", 6), ("Z1", 7), ("X2", 4), ("A4", 8),
-    ("H", 3), ("E1", 1), ("E2", 1), ("H", 2), ("X2", 5), ("M1", 8), ("Z1", 4), ("E3", 1),
-    ("M1", 9), ("Z1", 5), ("E1", 3), ("X2", 8), ("H", 7), ("M2", 1), ("H", 4), ("E1", 2),
-    ("E2", 2), ("E2", 3), ("X2", 9), ("Z1", 8), ("E1", 7), ("E3", 2), ("G2", 1), ("E1", 4),
-    ("H", 5), ("E3", 3), ("E2", 7), ("E2", 4), ("Z1", 9), ("H", 6), ("M2", 2), ("E1", 5),
-    ("H", 8), ("E2", 5), ("M2", 3), ("E3", 7), ("E3", 4), ("G2", 2), ("G4", 1), ("H", 9),
-    ("E1", 6), ("E2", 6), ("H", 10), ("G2", 3), ("E3", 5), ("E1", 8), ("M2", 7), ("E2", 8),
-    ("M2", 4), ("E3", 6), ("E1", 9), ("E2", 9), ("E1", 0), ("G2", 7), ("M2", 5), ("G2", 4),
-    ("E3", 8), ("G4", 2), ("E2", 0), ("M2", 6), ("E3", 9), ("E1", 10), ("E2", 10), ("G2", 5),
-    ("M2", 8), ("E3", 0), ("G2", 6), ("M2", 9), ("E3", 10), ("G4", 7), ("G2", 8), ("G4", 4),
-    ("M2", 0), ("G2", 9), ("G4", 3), ("G4", 5), ("G4", 6), ("G2", 0), ("G4", 8), ("G4", 9),
-    ("M2", 10), ("G2", 10), ("G4", 10), ("G4", 0),
+    (A2, 0), (A2, 1), (A2, 2), (A2, 13), (A4, 13), (M1, 13), (A4, 0), (A4, 1),
+    (M1, 0), (A2, 3), (A2, 5), (X2, 13), (A4, 2), (M1, 1), (M1, 2), (A2, 6),
+    (A4, 3), (X2, 0), (A2, 10), (A2, 4), (A2, 12), (X2, 1), (M1, 3), (X2, 2),
+    (A4, 5), (A4, 6), (Z1, 0), (Z1, 13), (A4, 10), (M1, 5), (A4, 4), (X2, 3),
+    (Z1, 1), (M1, 4), (A4, 12), (Z1, 2), (A2, 11), (A2, 7), (A2, 9), (Z1, 3),
+    (A2, 8), (X2, 5), (A4, 11), (M1, 10), (H, 13), (X2, 4), (Z1, 5), (H, 2),
+    (A4, 9), (M1, 6), (M1, 11), (X2, 10), (H, 3), (M1, 12), (Z1, 4), (X2, 11),
+    (E1, 2), (H, 5), (X2, 6), (E2, 2), (E1, 5), (M1, 9), (Z1, 10), (A4, 8),
+    (H, 4), (X2, 12), (M1, 8), (A4, 7), (Z1, 6), (X2, 9), (Z1, 11), (M1, 7),
+    (H, 10), (Z1, 12), (E2, 5), (E1, 3), (X2, 8), (E2, 3), (H, 6), (E3, 2),
+    (H, 11), (X2, 7), (Z1, 9), (Z1, 8), (E1, 4), (E3, 3), (E2, 4), (H, 12),
+    (M2, 2), (Z1, 7), (E3, 5), (E1, 10), (E2, 10), (E1, 11), (E2, 11), (M2, 3),
+    (G2, 2), (E3, 4), (H, 9), (E1, 12), (M2, 5), (E2, 12), (H, 8), (H, 0),
+    (E3, 10), (E3, 11), (E1, 6), (G2, 3), (H, 7), (E2, 6), (E1, 9), (M2, 4),
+    (E2, 9), (E1, 8), (G2, 5), (H, 1), (E3, 12), (M2, 10), (E2, 8), (M2, 11),
+    (E3, 6), (G2, 4), (E1, 7), (E3, 9), (G2, 10), (E2, 7), (E1, 0), (E2, 0),
+    (M2, 12), (G2, 11), (E3, 8), (E1, 1), (G4, 3), (M2, 6), (E2, 1), (G4, 2),
+    (M2, 9), (E3, 7), (G2, 12), (E3, 0), (G4, 4), (E1, 13), (G2, 6), (M2, 8),
+    (G2, 9), (E2, 13), (E3, 1), (G4, 10), (M2, 7), (G4, 5), (G2, 8), (M2, 0),
+    (G4, 12), (G4, 11), (G2, 7), (E3, 13), (M2, 1), (G2, 0), (G4, 6), (G4, 9),
+    (G2, 1), (G4, 8), (G4, 7), (M2, 13), (G2, 13), (G4, 13), (G4, 0), (G4, 1),
 )
-FIRST_UP = next(p for step, p in ORDER if step == "M1")
-FIRST_DOWN = next(p for step, p in ORDER if step == "M2")
+FIRST_UP = next(p for step, p in ORDER if step == M1)
+FIRST_DOWN = next(p for step, p in ORDER if step == M2)
 ARRIVALS = ("az", "ay", "ac", "s1", "lo", "z", "ez", "e1", "e2", "gc", "gy")
 SENDS = ("tokens", "sums", "hidden", "outputs")
+RECEIVE = {
+    key: i for i, key in enumerate(
+        [(p, name) for p, kind in enumerate(KIND) for name in ARRIVALS
+         if not (name == "az" and kind != SHIFTED or name in ("ay", "gy") and kind == HERE)]
+        + [(0, "last"), (1, "last")]
+    )
+}
 BUFFERS = (
     "tok", "part", "first", "second", "zsend", "zkeep", "zrecv", "hid", "outp", "crecv", "osum", "ysum", "zos"
 )
@@ -54,10 +71,10 @@
     ]
 
 
-def kernel(tokens_hbm, gate_hbm, up_hbm, down_hbm, out, tokens, wgu, wd, total, zor, *scratch):
+def kernel(tokens, gate_hbm, up_hbm, down_hbm, out, wgu, wd, total, zor, *scratch):
     big = dict(zip(BUFFERS, scratch))
     small = dict(zip(BUFFERS, scratch[len(BUFFERS):]))
-    send_sem, recv_sem, last_sem, weight_sem = scratch[2 * len(BUFFERS):]
+    send_sem, recv_sem, weight_sem = scratch[2 * len(BUFFERS):]
     gx, gy, gz = lax.axis_index("gx"), lax.axis_index("gy"), lax.axis_index("gz")
     x, h, y, c, zl = lax.rem(gz, 4), gz // 4, gx // 2, lax.rem(gx, 2), gy
     ff = gate_hbm.shape[1]
@@ -80,7 +97,7 @@
     zdown = [None, zup[3], zup[2], zup[1]]
 
     loads = [
-        pltpu.make_async_copy(tokens_hbm, tokens, weight_sem.at[3]),
+        pltpu.make_async_copy(tokens, panel(OWN, "tok").at[pl.ds(4 * c, 4)], weight_sem.at[3]),
         pltpu.make_async_copy(gate_hbm, wgu.at[:, pl.ds(0, ff)], weight_sem.at[0]),
         pltpu.make_async_copy(up_hbm, wgu.at[:, pl.ds(ff, ff)], weight_sem.at[1]),
         pltpu.make_async_copy(down_hbm, wd, weight_sem.at[2]),
@@ -93,16 +110,15 @@
         load.start()
     cy = 4 * c + y
     total[...] = jnp.zeros_like(total)
-    loads[0].wait()
     pl.semaphore_wait(barrier, len(peers))
 
     def arrival(p, name):
-        return recv_sem.at[p, ARRIVALS.index(name)] if name in ARRIVALS else last_sem.at[p]
+        return recv_sem.at[RECEIVE[p, name]]
 
     def send(p, group, name, src, dst, to):
         pltpu.make_async_remote_copy(
             src_ref=src, dst_ref=dst, send_sem=send_sem.at[2 if p == OWN else int(p in SMALL), SENDS.index(group)],
-            recv_sem=arrival(SHIFTED[p][1] // 32 if name == "last" else p, name),
+            recv_sem=arrival(PANELS[p][2] // 32 if name == "last" else p, name),
             device_id=to, device_id_type=pl.DeviceIdType.MESH,
         ).start()
 
@@ -115,15 +131,15 @@
     def flush():
         for i, name in enumerate(("tok", "part", "hid", "outp")):
             whole = name in ("tok", "outp")
-            blocks = pl.ds(0, 8 if whole else 7)
+            blocks, others = pl.ds(0, 8 if whole else 7), len(SMALL) - 1
             extents = (
-                big[name].at[:, blocks], small[name].at[pl.ds(0, 5), blocks],
-                small[name].at[5, pl.ds(0, 4 if whole else 7)],
+                big[name].at[:, blocks], small[name].at[pl.ds(0, others), blocks],
+                small[name].at[others, pl.ds(0, 4 if whole else 7)],
             )
             for k, extent in enumerate(extents):
                 pltpu.make_async_remote_copy(
                     src_ref=extent, dst_ref=extent, send_sem=send_sem.at[k, i],
-                    recv_sem=recv_sem.at[0, 0], device_id=core, device_id_type=pl.DeviceIdType.MESH,
+                    recv_sem=recv_sem.at[0], device_id=core, device_id_type=pl.DeviceIdType.MESH,
                 ).wait_send()
 
     g, u = pl.ds(0, ff), pl.ds(ff, ff)
@@ -137,22 +153,20 @@
     upper, lower = pl.ds(0, 2), pl.ds(2, 2)
 
     def a1(p):
-        offset, row, rows = SHIFTED[p]
+        _, offset, row, rows = PANELS[p]
         source = tokens.at[pl.ds(row // 16, 2)] if rows == 32 else tokens.at[row // 16]
         send(p, "tokens", "az", source, panel(p, "tok").at[cy], zdown[offset])
 
     def a2(p):
         tok = panel(p, "tok")
-        if p == OWN:
-            tok[pl.ds(4 * c, 4)] = tokens[...]
-        elif p == NEAR:
-            send(p, "tokens", "ay", tokens.at[upper], tok.at[pl.ds(4 * c + 2, 2)], yr)
-            send(p, "tokens", "ay", tokens.at[upper], tok.at[pl.ds(4 * c, 2)], yl)
-        elif p == MIDDLE:
-            send(p, "tokens", "ay", tokens.at[lower], tok.at[4 * c + 1], yr)
-            send(p, "tokens", "ay", tokens.at[lower], tok.at[4 * c], yl)
-            send(p, "tokens", "ay", tokens.at[upper], tok.at[4 * c + 2], yf)
-            send(p, "tokens", "ay", tokens.at[lower], tok.at[4 * c + 3], yf)
+        if KIND[p] == HERE:
+            loads[0].wait()
+        elif KIND[p] == NEAR:
+            mine = tokens.at[pl.ds(PANELS[p][2] // 16, 2)]
+            send(p, "tokens", "ay", mine, tok.at[pl.ds(4 * c + 2, 2)], yr)
+            send(p, "tokens", "ay", mine, tok.at[pl.ds(4 * c, 2)], yl)
+        elif KIND[p] == FAR:
+            send(p, "tokens", "ay", tokens, tok.at[pl.ds(4 * c, 4)], yf)
         else:
             here = tok.at[cy]
             arrived(p, "az", here)
@@ -163,7 +177,7 @@
     def a4(p):
         tok = panel(p, "tok")
         if p != OWN:
-            arrived(p, "ay", tok.at[pl.ds(0, 3 if p in SHIFTED else 4)])
+            arrived(p, "ay", tok.at[pl.ds(0, 3 if KIND[p] == SHIFTED else 4)])
         here = tok.at[pl.ds(4 * c, 4)]
         send(p, "tokens", "ac", here, here, core)
 
@@ -267,13 +281,11 @@
             total[...] += both.reshape(total.shape)
             return
         osum[...] = both.astype(BF16)
-        if p == NEAR:
+        if KIND[p] == NEAR:
             send(p, "outputs", "gy", osum.at[upper], ysum.at[upper], yr)
             send(p, "outputs", "gy", osum.at[lower], ysum.at[lower], yl)
-        elif p == MIDDLE:
-            send(p, "outputs", "gy", osum.at[lower], ysum.at[lower], yf)
-            send(p, "outputs", "gy", osum.at[0], ysum.at[0], yr)
-            send(p, "outputs", "gy", osum.at[1], ysum.at[1], yl)
+        elif KIND[p] == FAR:
+            send(p, "outputs", "gy", osum, ysum, yf)
         else:
             send(p, "outputs", "gy", osum.at[mod4(y + 2)], ysum.at[1], yf)
             send(p, "outputs", "gy", osum.at[mod4(y + 1)], ysum.at[0], yr)
@@ -281,15 +293,15 @@
 
     def g4(p):
         osum, ysum, zos = (panel(p, n) for n in ("osum", "ysum", "zos"))
-        if p == NEAR:
+        if KIND[p] == NEAR:
             arrived(p, "gy", ysum)
-            total[pl.ds(0, 32)] += (f32(ysum[upper]) + f32(ysum[lower])).reshape(32, total.shape[1])
-        elif p == MIDDLE:
+            rows = pl.ds(PANELS[p][2], 32)
+            total[rows] += (f32(ysum[upper]) + f32(ysum[lower])).reshape(32, total.shape[1])
+        elif KIND[p] == FAR:
             arrived(p, "gy", ysum)
-            total[pl.ds(0, 32)] += f32(ysum[2])
-            total[pl.ds(32, 32)] += f32(ysum[0]) + f32(ysum[1]) + f32(ysum[3])
-        elif p in SHIFTED:
-            offset, row, rows = SHIFTED[p]
+            total[...] += f32(ysum[...]).reshape(total.shape)
+        elif KIND[p] == SHIFTED:
+            _, offset, row, rows = PANELS[p]
             arrived(p, "gy", ysum.at[pl.ds(0, 3)])
             zos[...] = (f32(osum[y]) + f32(ysum[0]) + f32(ysum[1]) + f32(ysum[2])).astype(BF16)
             there = zor.at[row // 32, offset - 1, pl.ds(row % 32, rows)]
@@ -301,10 +313,11 @@
         whole = total[rows] + f32(zor[q, 0]) + f32(zor[q, 1]) + f32(zor[q, 2])
         out[rows, :] = whole.astype(BF16)
 
-    steps = dict(A2=a2, A4=a4, M1=m1, X2=x2, Z1=z1, H=hidden, E1=e1, E2=e2, E3=e3, M2=m2, G2=g2, G4=g4)
+    steps = (a2, a4, m1, x2, z1, hidden, e1, e2, e3, m2, g2, g4)
     steps[ORDER[0][0]](ORDER[0][1])
-    for p in SHIFTED:
-        a1(p)
+    for p, kind in enumerate(KIND):
+        if kind == SHIFTED:
+            a1(p)
     for step, p in ORDER[1:]:
         steps[step](p)
     g5(0)
@@ -317,7 +330,6 @@
     quarters = tokens.reshape(4, 16, depth)
     wide = down_weight.shape[1]
     scratch = [
-        pltpu.VMEM(quarters.shape, BF16),
         pltpu.VMEM((depth, 2 * ff), BF16),
         pltpu.VMEM((ff, wide), BF16),
         pltpu.VMEM(tokens.shape, F32),
@@ -326,8 +338,7 @@
     scratch += buffers(len(BIG), (2, 16), depth, ff, wide) + buffers(len(SMALL), (16,), depth, ff, wide)
     scratch += [
         pltpu.SemaphoreType.DMA((3, len(SENDS))),
-        pltpu.SemaphoreType.DMA((PANELS, len(ARRIVALS))),
-        pltpu.SemaphoreType.DMA((2,)),
+        pltpu.SemaphoreType.DMA((len(RECEIVE),)),
         pltpu.SemaphoreType.DMA((4,)),
     ]
     whole = pl.BlockSpec(memory_space=pltpu.VMEM)

time: 121 us -> 118 us (0.975)
  Pallas kernels: 120 us -> 117 us
    pallas_call x1, Pallas kernels: 120 us -> 117 us  [shards(): pl.pallas_call(kernel, out_shape=jax.ShapeDtypeStruct(tokens.shape, BF16)...]
where the time goes in v4:
time: 118 us
  Pallas kernels  117 us (99%)
  local copies, waits for them, and re-layouts  1.57 us (1%)
    pallas_call x1, Pallas kernels, shards(): pl.pallas_call(kernel, out_shape=jax.ShapeDtypeStruct(tokens.shape, BF16)...  117 us

profile of v4, /device:TPU:1, one launch (start us, length us, event | category | flops | bytes accessed | tf_op | source)
XLA Modules:
  0.0 118.1 jit_solution(14060323394809070760)
XLA Ops:
  0.0 116.5 %swiglu.1 = bf16[64,1024]{1,0:T(8,128)(2,1)} custom-call(bf16[4,16,1024]{2,1,0:T(8,128)(2,1)} %bitcast.1, bf16[1024,896]{1,0:T(8,128)(2,1)} %gate_hbm.1, bf16[1024,896]{1,0:T(8,128)(2,1)} %up_hbm.1, bf16[896,1024]{1,0:T(8,128)(2,1)} %down_hbm.1), custom_call_target="tpu_custom_call" | custom-call | tf_op jit(solution)/shard_map/swiglu/pallas_call | solution.py:346
  116.5 1.6 %copy.6 = bf16[64,1024]{1,0:T(8,128)(2,1)} copy(bf16[64,1024]{1,0:T(8,128)(2,1)} %swiglu.1) | data formatting | bytes 262144

commit v5 on v4

--- a/solution.py
+++ b/solution.py
@@ -71,7 +71,7 @@
     ]
 
 
-def kernel(tokens, gate_hbm, up_hbm, down_hbm, out, wgu, wd, total, zor, *scratch):
+def kernel(tokens, gate_hbm, up_hbm, down_hbm, out_hbm, out, wgu, wd, total, zor, *scratch):
     big = dict(zip(BUFFERS, scratch))
     small = dict(zip(BUFFERS, scratch[len(BUFFERS):]))
     send_sem, recv_sem, weight_sem = scratch[2 * len(BUFFERS):]
@@ -312,6 +312,7 @@
         rows = pl.ds(32 * q, 32)
         whole = total[rows] + f32(zor[q, 0]) + f32(zor[q, 1]) + f32(zor[q, 2])
         out[rows, :] = whole.astype(BF16)
+        pltpu.make_async_copy(out.at[rows], out_hbm.at[rows], weight_sem.at[4 + q]).start()
 
     steps = (a2, a4, m1, x2, z1, hidden, e1, e2, e3, m2, g2, g4)
     steps[ORDER[0][0]](ORDER[0][1])
@@ -323,6 +324,9 @@
     g5(0)
     g5(1)
     flush()
+    for q in (0, 1):
+        rows = pl.ds(32 * q, 32)
+        pltpu.make_async_copy(out.at[rows], out_hbm.at[rows], weight_sem.at[4 + q]).wait()
 
 
 def shards(tokens, gate_weight, up_weight, down_weight):
@@ -330,6 +334,7 @@
     quarters = tokens.reshape(4, 16, depth)
     wide = down_weight.shape[1]
     scratch = [
+        pltpu.VMEM(tokens.shape, BF16),
         pltpu.VMEM((depth, 2 * ff), BF16),
         pltpu.VMEM((ff, wide), BF16),
         pltpu.VMEM(tokens.shape, F32),
@@ -339,15 +344,14 @@
     scratch += [
         pltpu.SemaphoreType.DMA((3, len(SENDS))),
         pltpu.SemaphoreType.DMA((len(RECEIVE),)),
-        pltpu.SemaphoreType.DMA((4,)),
+        pltpu.SemaphoreType.DMA((6,)),
     ]
-    whole = pl.BlockSpec(memory_space=pltpu.VMEM)
     anywhere = pl.BlockSpec(memory_space=pl.ANY)
     return pl.pallas_call(
         kernel,
         out_shape=jax.ShapeDtypeStruct(tokens.shape, BF16),
         in_specs=[anywhere] * 4,
-        out_specs=whole,
+        out_specs=anywhere,
         scratch_shapes=scratch,
         compiler_params=pltpu.CompilerParams(
             collective_id=0, has_side_effects=True, vmem_limit_bytes=60 << 20

time: 118 us -> 117 us (level)
  no operation moved by 1% of the time
where the time goes in v5:
time: 117 us
  Pallas kernels  116 us (99%)
  local copies, waits for them, and re-layouts  1.57 us (1%)
    pallas_call x1, Pallas kernels, shards(): pl.pallas_call(kernel, out_shape=jax.ShapeDtypeStruct(tokens.shape, BF16)...  116 us

profile of v5, /device:TPU:1, one launch (start us, length us, event | category | flops | bytes accessed | tf_op | source)
XLA Modules:
  0.0 117.3 jit_solution(17637566418349215059)
XLA Ops:
  0.0 115.8 %swiglu.1 = bf16[64,1024]{1,0:T(8,128)(2,1)} custom-call(bf16[4,16,1024]{2,1,0:T(8,128)(2,1)} %bitcast.1, bf16[1024,896]{1,0:T(8,128)(2,1)} %gate_hbm.1, bf16[1024,896]{1,0:T(8,128)(2,1)} %up_hbm.1, bf16[896,1024]{1,0:T(8,128)(2,1)} %down_hbm.1), custom_call_target="tpu_custom_call" | custom-call | tf_op jit(solution)/shard_map/swiglu/pallas_call | solution.py:350
  115.8 1.6 %copy.6 = bf16[64,1024]{1,0:T(8,128)(2,1)} copy(bf16[64,1024]{1,0:T(8,128)(2,1)} %swiglu.1) | data formatting | bytes 262144
